TPU v7x, 256 devices: a whole 4x4x8 slice. The times are simulated.
256 devices in a mesh: space: 32 (over y, x, z_hi), band: 8 (over z_lo, core).
Axes of the slice: x: 4, y: 4, z: 8 (z_hi: 2, z_lo: 4; z = z_hi * 4 + z_lo), core: 2. Of those that a mesh axis runs over, the one named last changes fastest.
Arguments:
- orbitals: float32 [64, 192, 32, 128], P('band', 'space'), may hold values from -18 to 18
- previous: float32 [64, 192, 32, 128], P('band', 'space'), may hold values from -18 to 18
- potential: float32 [192, 32, 128], P('space'), may hold values from -4 to 4
- projectors: bfloat16 [128, 9, 6, 32, 128], P('space'), may hold values from -0.1875 to 0.1875
- strengths: float32 [128, 9], replicated, may hold values from -3 to 3
- atom_planes: int32 [128], replicated, may hold values from 0 to 191, as said below
Outputs:
- filtered: bfloat16 [64, 192, 32, 128], P('band', 'space')
- margin: float32 [64, 64], P('space', 'band')
- projection: float32 [64, 64], P('space', 'band')
Inputs may be any that keep to these rules, and one draw needn't show every extreme that they name: `atom_planes`: entry a is the first plane of atom a's box of 6 planes. In each aligned block of 4 entries (block s) every box starts at one of the planes s * 6 to s * 6 + 5, and in every block one atom starts at the first of these planes and another at the last.
All inputs are finite; a program needn't handle non-finite values.
Results may differ from a plain program's by a relative error of at most 0.0065.
Values may be sent and summed in bfloat16 or wider, within the bound.
A program may use at most 192 MiB of HBM per device.

v0:
```python
import jax
import jax.numpy as jnp
from jax import lax
from jax.sharding import PartitionSpec as P

HALO = 6
BOX = 6
NPJ = 9
stencil_weights = (
    -5369.0 / 1800.0,
    12.0 / 7.0,
    -15.0 / 56.0,
    10.0 / 189.0,
    -1.0 / 112.0,
    2.0 / 1925.0,
    -1.0 / 16632.0,
)
center = 5.5
halfwidth = 5.5


def with_halo(block, sides, width):
    for axis, dim in sides:
        count = lax.axis_size(axis)
        forward = [(i, i + 1) for i in range(count - 1)]
        forward.append((count - 1, 0))
        backward = [(target, source) for source, target in forward]
        low = lax.ppermute(
            lax.slice_in_dim(block, block.shape[dim] - width, None, axis=dim), axis, forward
        )
        high = lax.ppermute(lax.slice_in_dim(block, 0, width, axis=dim), axis, backward)
        block = jnp.concatenate([low, block, high], axis=dim)
    return block


def shifted(value, axis, steps):
    count = lax.axis_size(axis)
    pairs = [(source, (source + steps) % count) for source in range(count)]
    return lax.ppermute(value, axis, pairs)


def laplace_axis(field, axis):
    total = stencil_weights[0] * field
    for offset in range(1, HALO + 1):
        total = total + stencil_weights[offset] * (
            jnp.roll(field, offset, axis) + jnp.roll(field, -offset, axis)
        )
    return total


def place_table(first_planes, projector_block, base, window, total_planes):
    box_rows = jnp.arange(BOX, dtype=jnp.int32)
    planes_out = jnp.arange(window, dtype=jnp.int32)
    relative = (first_planes[:, None] + box_rows[None, :] - base) % total_planes
    placer = (planes_out[None, None, :] == relative[:, :, None]).astype(jnp.float32)
    return jnp.einsum(
        "apq,ajpyz->ajqyz",
        placer,
        projector_block.astype(jnp.float32),
        precision=lax.Precision.HIGHEST,
    )


def shards(orbitals, previous, potential, projectors, strengths, atom_planes):
    band_dev, slab_planes, cells_y, cells_z = orbitals.shape
    space_count = lax.axis_size("space")
    total_planes = slab_planes * space_count
    extended = with_halo(orbitals, (("space", 1),), HALO)
    along_x = stencil_weights[0] * orbitals
    for offset in range(1, HALO + 1):
        ahead = extended[:, HALO + offset : HALO + offset + slab_planes]
        behind = extended[:, HALO - offset : HALO - offset + slab_planes]
        along_x = along_x + stencil_weights[offset] * (ahead + behind)
    kinetic = -0.5 * (along_x + laplace_axis(orbitals, 2) + laplace_axis(orbitals, 3))
    device_index = lax.axis_index("space")
    atom_count = projectors.shape[0]
    own_start = device_index * atom_count
    own_planes = lax.dynamic_slice_in_dim(atom_planes, own_start, atom_count, 0)
    own_strengths = lax.dynamic_slice_in_dim(strengths, own_start, atom_count, 0)
    table = place_table(
        own_planes, projectors, device_index * slab_planes, slab_planes + HALO, total_planes
    )
    table_flat = table.reshape(atom_count * NPJ, -1)
    upper = extended[:, HALO:].reshape(band_dev, -1)
    coefficients = lax.dot_general(
        table_flat,
        upper,
        (((1,), (1,)), ((), ())),
        precision=lax.Precision.HIGHEST,
        preferred_element_type=jnp.float32,
    )
    weighted = coefficients * own_strengths.reshape(-1)[:, None]
    added = lax.dot_general(
        weighted,
        table_flat,
        (((0,), (0,)), ((), ())),
        precision=lax.Precision.HIGHEST,
        preferred_element_type=jnp.float32,
    )
    added = added.reshape(band_dev, slab_planes + HALO, cells_y, cells_z)
    arrived = shifted(added[:, slab_planes:].astype(jnp.bfloat16), "space", 1).astype(jnp.float32)
    padding = jnp.zeros((band_dev, slab_planes - HALO, cells_y, cells_z), jnp.float32)
    projected_term = added[:, :slab_planes] + jnp.concatenate([arrived, padding], 1)
    hamil = kinetic + potential[None] * orbitals + projected_term
    filtered = (2.0 / halfwidth * (hamil - center * orbitals) - previous).astype(jnp.bfloat16)
    scale = 1.0 / (slab_planes * space_count * cells_y * cells_z)
    filtered_flat = filtered.reshape(band_dev, -1)
    panel_flat = orbitals.astype(jnp.bfloat16).reshape(band_dev, -1)
    columns_right = jnp.concatenate([filtered_flat, panel_flat], 0)
    piece = lax.all_gather(filtered, "band", axis=0, tiled=True)
    rows = piece.reshape(piece.shape[0], -1)
    products = lax.dot_general(
        rows, columns_right, (((1,), (1,)), ((), ())), preferred_element_type=jnp.float32
    )
    partial_sums = products * scale
    shares = lax.psum_scatter(partial_sums, "space", scatter_dimension=0, tiled=True)
    margin = shares[:, :band_dev]
    projection = shares[:, band_dev:]
    return (filtered, margin, projection)


def solution(mesh):
    in_specs = (
        P("band", "space", None, None),
        P("band", "space", None, None),
        P("space", None, None),
        P("space", None, None, None, None),
        P(),
        P(),
    )
    out_specs = (P("band", "space", None, None), P("space", "band"), P("space", "band"))
    return jax.shard_map(shards, mesh=mesh, in_specs=in_specs, out_specs=out_specs, check_vma=False)
```

profile of v0, /device:TPU:32, one launch (start us, length us, event | category | flops | bytes accessed | tf_op | source)
XLA Modules:
  0.0 414.5 jit_solution(45234726132586732)
XLA Ops:
  7.2 1.7 copy.130
  8.9 6.4 %collective-permute-start.1 = (f32[8,6,32,128]{3,0,2,1:T(8,128)S(1)}, f32[8,6,32,128]{3,0,2,1:T(8,128)S(1)}, u32[]{:S(2)}, u32[]{:S(2)}) collective-permute-start(f32[8,6,32,128]{3,0,2,1:T(8,128)S(1)} %copy.130), channel_id=1, source_target_pairs={{0,8},{8,16},{16,24},{24,32},{32,40},{40,48},{48,56},{56,64},{64,7... | collective-permute-start | bytes 2359304 | tf_op jit(solution)/shard_map/ppermute | solution.py:28
  15.3 4.7 %collective-permute-start = (f32[8,6,32,128]{3,0,2,1:T(8,128)S(1)}, f32[8,6,32,128]{3,0,2,1:T(8,128)}, u32[]{:S(2)}, u32[]{:S(2)}) collective-permute-start(f32[8,6,32,128]{3,0,2,1:T(8,128)S(1)} %copy.130), channel_id=1, source_target_pairs={{8,0},{16,8},{24,16},{32,24},{40,32},{48,40},{56,48},{64,56},{72,6... | collective-permute-start | bytes 2359304 | tf_op jit(solution)/shard_map/ppermute | solution.py:31
  31.3 1.4 fusion.75
  32.8 1.5 fusion.72
  34.2 1.4 fusion.73
  41.3 1.5 fusion.66
  43.0 1.7 convolution_bitcast_fusion
  44.7 5.9 %copy.185 = f32[4,9,12,32,128]{4,3,2,1,0:T(8,128)} copy(f32[4,9,12,32,128]{4,2,3,1,0:T(8,128)S(1)} %convolution_bitcast_fusion) | data formatting | bytes 14155776 | tf_op jit(solution)/shard_map/apq,ajpyz->ajqyz/transpose | solution.py:56
  50.7 7.8 %reshape.53 = f32[36,49152]{1,0:T(8,128)} reshape(f32[4,9,12,32,128]{4,3,2,1,0:T(8,128)} %copy.185) | data formatting | bytes 14155776 | tf_op jit(solution)/shard_map/reshape | solution.py:83
  58.4 1.5 fusion.67
  60.2 4.7 %copy.194 = f32[5,8,384,128]{3,2,1,0:T(8,128)S(1)} copy(f32[5,8,384,128]{3,1,2,0:T(8,128)} %bitcast.38) | data formatting | bytes 15728640
  67.0 1.6 collective-permute-done.1
  69.1 3.2 collective-permute-done
  73.5 6.2 %fusion.9 = f32[36,8,1,1]{0,1,3,2:T(8,128)S(1)} fusion(f32[36,49152]{1,0:T(8,128)S(1)} %bitcast.40, f32[8,49152]{1,0:T(8,128)S(1)} %bitcast.43, f32[36]{0:T(128)S(1)} %mul.132), kind=kOutput, calls=%fused_computation.9 | convolution fusion | flops 169869600 | bytes 8652048 | tf_op jit(solution)/shard_map/dot_general | solution.py:85
  79.8 8.1 %fusion = f32[8,12,32,128]{3,0,2,1:T(8,128)S(1)} fusion(f32[36,8,1,1]{0,1,3,2:T(8,128)S(1)} %fusion.9, f32[12,32,128,36]{2,1,0,3:T(8,128)S(1)} %bitcast.41), kind=kOutput, calls=%fused_computation | convolution fusion | flops 169869312 | bytes 8651904 | tf_op jit(solution)/shard_map/dot_general | solution.py:93
  87.9 6.3 %collective-permute-start.2 = (bf16[8,6,32,128]{3,0,2,1:T(8,128)(2,1)S(1)}, bf16[8,6,32,128]{3,0,2,1:T(8,128)(2,1)}, u32[]{:S(2)}, u32[]{:S(2)}) collective-permute-start(bf16[8,6,32,128]{3,0,2,1:T(8,128)(2,1)S(1)} %slice.432), channel_id=1, source_target_pairs={{0,8},{8,16},{16,24},{24,32},{32,40},{40,48},{48,56},{56,64},{64,7... | collective-permute-start | bytes 1179656 | tf_op jit(solution)/shard_map/ppermute | solution.py:39
  94.2 1.5 fusion.65
  95.7 16.5 %collective-permute-done.2 = bf16[8,6,32,128]{3,0,2,1:T(8,128)(2,1)} collective-permute-done((bf16[8,6,32,128]{3,0,2,1:T(8,128)(2,1)S(1)}, bf16[8,6,32,128]{3,0,2,1:T(8,128)(2,1)}, u32[]{:S(2)}, u32[]{:S(2)}) %collective-permute-start.2) | collective-permute-done | bytes 393248 | tf_op jit(solution)/shard_map/ppermute | solution.py:39
  112.3 12.4 %fusion.14 = bf16[8,6,32,128]{3,0,2,1:T(8,128)(2,1)} fusion(f32[8,12,32,128]{3,0,2,1:T(8,128)S(1)} %fusion, f32[8,12,32,128]{3,0,2,1:T(8,128)S(1)} %get-tuple-element.60, f32[8,12,32,128]{3,0,2,1:T(8,128)S(1)} %constant_dynamic-update-slice_fusion, f32[8,6,31,128]{3,0,2,1:T(8,128)} %get-tuple-element.57, f32[8,6,1,128]{3,0,2,1:T(8,128)S(1)} %get-tuple-element.59, ...), kind=kLoop, calls=%fused_computation.16 | loop fusion | flops 18087936 | bytes 31555584 | tf_op jit(solution)/shard_map/convert_element_type | solution.py:105
  127.4 50.6 %all-gather.2.cloned.1.call-done = bf16[64,6,32,128]{3,0,2,1:T(8,128)(2,1)} async-done(((bf16[8,6,32,128]{3,0,2,1:T(8,128)(2,1)}), bf16[64,6,32,128]{3,0,2,1:T(8,128)(2,1)}) %all-gather.2.cloned.1.call-update) | async-done | bytes 3145744 | tf_op jit(solution)/shard_map/all_gather | solution.py:110
  178.0 3.9 copy.190
  181.9 1.8 fusion.6
  183.8 223.2 %all-reduce = f32[64,16]{1,0:T(8,128)S(1)} all-reduce(f32[64,16]{1,0:T(8,128)S(1)} %fusion.6), channel_id=2, replica_groups=mesh['space'=32,'band'=8] {'space'}, use_global_device_ids=true, to_apply=%region_0.1.clone | all-reduce | flops 1024 | bytes 8192
  (67 shorter events, 24.0 us)
Async XLA Ops:
  7.2 35.8 %copy-start = (bf16[4,9,6,32,128]{4,3,2,1,0:T(8,128)(2,1)S(1)}, bf16[4,9,6,32,128]{4,3,2,1,0:T(8,128)(2,1)}, u32[]{:S(2)}) copy-start(bf16[4,9,6,32,128]{4,3,2,1,0:T(8,128)(2,1)} %param.9) | copy-start | bytes 5308420
  7.2 170.8 %all-gather.2.cloned.1.call-start = ((), (), s32[]{:S(2)}) async-start(), calls=%async_computation | async-start | bytes 3538944 | tf_op jit(solution)/shard_map/all_gather | solution.py:110
  8.9 59.7 %collective-permute-start.1 = (f32[8,6,32,128]{3,0,2,1:T(8,128)S(1)}, f32[8,6,32,128]{3,0,2,1:T(8,128)S(1)}, u32[]{:S(2)}, u32[]{:S(2)}) collective-permute-start(f32[8,6,32,128]{3,0,2,1:T(8,128)S(1)} %copy.130), channel_id=1, source_target_pairs={{0,8},{8,16},{16,24},{24,32},{32,40},{40,48},{48,56},{56,64},{64,7... | collective-permute-start | bytes 2359304 | tf_op jit(solution)/shard_map/ppermute | solution.py:28
  15.3 57.0 %collective-permute-start = (f32[8,6,32,128]{3,0,2,1:T(8,128)S(1)}, f32[8,6,32,128]{3,0,2,1:T(8,128)}, u32[]{:S(2)}, u32[]{:S(2)}) collective-permute-start(f32[8,6,32,128]{3,0,2,1:T(8,128)S(1)} %copy.130), channel_id=1, source_target_pairs={{8,0},{16,8},{24,16},{32,24},{40,32},{48,40},{56,48},{64,56},{72,6... | collective-permute-start | bytes 2359304 | tf_op jit(solution)/shard_map/ppermute | solution.py:31
  41.3 1.5 copy-start.11
  58.4 1.5 copy-start.10
  64.8 8.7 %slice-start = ((s8[7864320]{0:T(1024)(128)(4,1)}), s8[4194304]{0:T(1024)(128)(4,1)S(1)}, s32[]{:S(2)}) async-start(s8[7864320]{0:T(1024)(128)(4,1)} %bitcast.39), calls=%async_computation.1 | async-start | bytes 8388608
  64.8 8.7 %slice-start.1 = ((s8[7864320]{0:T(1024)(128)(4,1)}), s8[3670016]{0:T(1024)(128)(4,1)S(1)}, s32[]{:S(2)}) async-start(s8[7864320]{0:T(1024)(128)(4,1)} %bitcast.39), calls=%async_computation.2 | async-start | bytes 7340032
  65.6 3.1 copy-start.2
  87.8 24.4 %copy-start.8 = (f32[8,6,32,126]{3,0,2,1:T(8,128)S(1)}, f32[8,6,32,126]{3,0,2,1:T(8,128)}, u32[]{:S(2)}) copy-start(f32[8,6,32,126]{3,0,2,1:T(8,128)} %get-tuple-element.28) | copy-start | bytes 2322436
  87.9 24.3 %copy-start.4 = (f32[8,6,32,127]{3,0,2,1:T(8,128)S(1)}, f32[8,6,32,127]{3,0,2,1:T(8,128)}, u32[]{:S(2)}) copy-start(f32[8,6,32,127]{3,0,2,1:T(8,128)} %get-tuple-element.32) | copy-start | bytes 2340868
  87.9 24.3 %copy-start.5 = (f32[8,6,32,127]{3,0,2,1:T(8,128)S(1)}, f32[8,6,32,127]{3,0,2,1:T(8,128)}, u32[]{:S(2)}) copy-start(f32[8,6,32,127]{3,0,2,1:T(8,128)} %get-tuple-element.33) | copy-start | bytes 2340868
  87.9 24.3 %copy-start.6 = (f32[8,6,32,1]{3,0,2,1:T(8,128)S(1)}, f32[8,6,32,1]{3,0,2,1:T(8,128)}, u32[]{:S(2)}) copy-start(f32[8,6,32,1]{3,0,2,1:T(8,128)} %get-tuple-element.34) | copy-start | bytes 18436
  87.9 24.3 %copy-start.7 = (f32[8,6,32,1]{3,0,2,1:T(8,128)S(1)}, f32[8,6,32,1]{3,0,2,1:T(8,128)}, u32[]{:S(2)}) copy-start(f32[8,6,32,1]{3,0,2,1:T(8,128)} %get-tuple-element.35) | copy-start | bytes 18436
  87.9 24.3 %copy-start.9 = (f32[8,6,6,128]{3,0,2,1:T(8,128)S(1)}, f32[8,6,6,128]{3,0,2,1:T(8,128)}, u32[]{:S(2)}) copy-start(f32[8,6,6,128]{3,0,2,1:T(8,128)} %get-tuple-element.39) | copy-start | bytes 442372
  87.9 24.3 %collective-permute-start.2 = (bf16[8,6,32,128]{3,0,2,1:T(8,128)(2,1)S(1)}, bf16[8,6,32,128]{3,0,2,1:T(8,128)(2,1)}, u32[]{:S(2)}, u32[]{:S(2)}) collective-permute-start(bf16[8,6,32,128]{3,0,2,1:T(8,128)(2,1)S(1)} %slice.432), channel_id=1, source_target_pairs={{0,8},{8,16},{16,24},{24,32},{32,40},{40,48},{48,56},{56,64},{64,7... | collective-permute-start | bytes 1179656 | tf_op jit(solution)/shard_map/ppermute | solution.py:39
  124.6 0.7 copy-start.12
  124.6 1.9 copy-start.3
  181.9 225.7 %copy-start.1 = (bf16[4,9,6,32,128]{4,3,2,1,0:T(8,128)(2,1)S(1)}, bf16[4,9,6,32,128]{4,3,2,1,0:T(8,128)(2,1)}, u32[]{:S(2)}) copy-start(bf16[4,9,6,32,128]{4,3,2,1,0:T(8,128)(2,1)} %param.9) | copy-start | bytes 5308420
Sparse Core Ops, SparseCore 0:
  124.8 53.1 all-gather.1
where the time goes:
time: 415 us; the launch traced here: 414 us
  blocking collectives  223 us (54%)
  waiting for transfers between devices  72 us (17%)
  local copies, waits for them, and re-layouts  56.6 us (14%)
  matrix products  17.9 us (4%)
  starting transfers between devices  17.4 us (4%)
  between operations  15 us (4%)
  other arithmetic  12.5 us (3%)
    unnamed x1, blocking collectives  223 us
    all_gather x1, waiting for transfers between devices, shards(): piece = lax.all_gather(filtered, 'band', axis=0, tiled=True)  50.6 us
    slice x24, local copies, waits for them, and re-layouts, laplace_axis(): jnp.roll(field, -offset, axis)  27.1 us
    ppermute x1, waiting for transfers between devices, shifted(): return lax.ppermute(value, axis, pairs)  16.5 us
    convert_element_type x1, other arithmetic, shards(): (2.0 / halfwidth * (hamil - center * orbitals) - previous).astype(jnp.bfl...  12.4 us
    unnamed x38, local copies, waits for them, and re-layouts  9.18 us
  transfers between devices with their start and end apart: 4, of which 4 were waited for; matrix products, arithmetic and copies ran while one was open for 12% of the time, Pallas kernels for 0%

commit v1 on v0

--- a/solution.py
+++ b/solution.py
@@ -1,3 +1,4 @@
+import functools
 import jax
 import jax.numpy as jnp
 from jax import lax
@@ -17,6 +18,16 @@
 )
 center = 5.5
 halfwidth = 5.5
+
+
+def _refer_patch(my_tile, ax_name):
+    big = lax.axis_size(ax_name)
+    tmp = jnp.stack(big * [my_tile], axis=0)
+    reply = lax.all_to_all(tmp, ax_name, 0, 0)
+    return jnp.concatenate(reply, axis=0)
+
+
+_compute_roots = functools.partial(_refer_patch, ax_name="band")
 
 
 def with_halo(block, sides, width):
@@ -107,7 +118,7 @@
     filtered_flat = filtered.reshape(band_dev, -1)
     panel_flat = orbitals.astype(jnp.bfloat16).reshape(band_dev, -1)
     columns_right = jnp.concatenate([filtered_flat, panel_flat], 0)
-    piece = lax.all_gather(filtered, "band", axis=0, tiled=True)
+    piece = _compute_roots(filtered)
     rows = piece.reshape(piece.shape[0], -1)
     products = lax.dot_general(
         rows, columns_right, (((1,), (1,)), ((), ())), preferred_element_type=jnp.float32

time: 415 us -> 437 us (1.053)
  starting transfers between devices: 17.4 us -> 33.9 us
  waiting for transfers between devices: 72 us -> 87.4 us
  between operations: 15 us -> 1.55 us
    all_to_all x0 -> x1, waiting for transfers between devices: none -> 66.2 us  [_refer_patch(): reply = lax.all_to_all(tmp, ax_name, 0, 0)]
    all_gather x1 -> x0, waiting for transfers between devices: 50.6 us -> none  [shards(): piece = lax.all_gather(filtered, 'band', axis=0, tiled=True)]
    all_to_all x0 -> x1, starting transfers between devices: none -> 16.5 us  [_refer_patch(): reply = lax.all_to_all(tmp, ax_name, 0, 0)]
    another operation x0 -> x2, local copies, waits for them, and re-layouts: none -> 7.2 us  [the longest x1 4.75 us: shards(): rows = piece.reshape(piece.shape[0], -1)]
    unnamed x38 -> x40, local copies, waits for them, and re-layouts: 9.18 us -> 9.22 us
  transfers between devices with their start and end apart: 4 -> 4, of which waited for: 4 -> 4; matrix products, arithmetic and copies ran while one was open for 12% -> 11% of each run, Pallas kernels for 0% -> 0%
where the time goes in v1:
time: 437 us; the launch traced here: 434 us
  blocking collectives  221 us (51%)
  waiting for transfers between devices  87.4 us (20%)
  local copies, waits for them, and re-layouts  59.9 us (14%)
  starting transfers between devices  33.9 us (8%)
  matrix products  19 us (4%)
  other arithmetic  12 us (3%)
    unnamed x1, blocking collectives  221 us
    all_to_all x1, waiting for transfers between devices, _refer_patch(): reply = lax.all_to_all(tmp, ax_name, 0, 0)  66.2 us
    slice x24, local copies, waits for them, and re-layouts, laplace_axis(): jnp.roll(field, -offset, axis)  27.1 us
    all_to_all x1, starting transfers between devices, _refer_patch(): reply = lax.all_to_all(tmp, ax_name, 0, 0)  16.5 us
    ppermute x1, waiting for transfers between devices, shifted(): return lax.ppermute(value, axis, pairs)  16.4 us
    convert_element_type x1, other arithmetic, shards(): (2.0 / halfwidth * (hamil - center * orbitals) - previous).astype(jnp.bfl...  11.9 us
    unnamed x40, local copies, waits for them, and re-layouts  9.22 us
  transfers between devices with their start and end apart: 4, of which 4 were waited for; matrix products, arithmetic and copies ran while one was open for 11% of the time, Pallas kernels for 0%

profile of v1, /device:TPU:32, one launch (start us, length us, event | category | flops | bytes accessed | tf_op | source)
XLA Modules:
  0.0 434.2 jit_solution(15196816345287288907)
XLA Ops:
  0.6 1.7 copy.131
  2.4 6.4 %collective-permute-start.1 = (f32[8,6,32,128]{3,0,2,1:T(8,128)S(1)}, f32[8,6,32,128]{3,0,2,1:T(8,128)S(1)}, u32[]{:S(2)}, u32[]{:S(2)}) collective-permute-start(f32[8,6,32,128]{3,0,2,1:T(8,128)S(1)} %copy.131), channel_id=1, source_target_pairs={{0,8},{8,16},{16,24},{24,32},{32,40},{40,48},{48,56},{56,64},{64,7... | collective-permute-start | bytes 2359304 | tf_op jit(solution)/shard_map/ppermute | solution.py:39
  8.7 4.7 %collective-permute-start = (f32[8,6,32,128]{3,0,2,1:T(8,128)S(1)}, f32[8,6,32,128]{3,0,2,1:T(8,128)}, u32[]{:S(2)}, u32[]{:S(2)}) collective-permute-start(f32[8,6,32,128]{3,0,2,1:T(8,128)S(1)} %copy.131), channel_id=1, source_target_pairs={{8,0},{16,8},{24,16},{32,24},{40,32},{48,40},{56,48},{64,56},{72,6... | collective-permute-start | bytes 2359304 | tf_op jit(solution)/shard_map/ppermute | solution.py:42
  26.2 1.5 fusion.66
  34.8 1.5 fusion.60
  36.4 1.7 convolution_bitcast_fusion
  38.2 5.9 %copy.186 = f32[4,9,12,32,128]{4,3,2,1,0:T(8,128)} copy(f32[4,9,12,32,128]{4,2,3,1,0:T(8,128)S(1)} %convolution_bitcast_fusion) | data formatting | bytes 14155776 | tf_op jit(solution)/shard_map/apq,ajpyz->ajqyz/transpose | solution.py:67
  44.1 7.8 %reshape.52 = f32[36,49152]{1,0:T(8,128)} reshape(f32[4,9,12,32,128]{4,3,2,1,0:T(8,128)} %copy.186) | data formatting | bytes 14155776 | tf_op jit(solution)/shard_map/reshape | solution.py:94
  51.9 1.5 fusion.61
  53.6 4.7 %copy.195 = f32[5,8,384,128]{3,2,1,0:T(8,128)S(1)} copy(f32[5,8,384,128]{3,1,2,0:T(8,128)} %bitcast.34) | data formatting | bytes 15728640
  60.4 1.6 collective-permute-done.1
  62.6 3.2 collective-permute-done
  67.0 6.2 %fusion.3 = f32[36,8,1,1]{0,1,3,2:T(8,128)S(1)} fusion(f32[36,49152]{1,0:T(8,128)S(1)} %bitcast.36, f32[8,49152]{1,0:T(8,128)S(1)} %bitcast.39, f32[36]{0:T(128)S(1)} %mul.132), kind=kOutput, calls=%fused_computation.6 | convolution fusion | flops 169869600 | bytes 8652048 | tf_op jit(solution)/shard_map/dot_general | solution.py:96
  73.2 8.1 %fusion = f32[8,12,32,128]{3,0,2,1:T(8,128)S(1)} fusion(f32[36,8,1,1]{0,1,3,2:T(8,128)S(1)} %fusion.3, f32[12,32,128,36]{2,1,0,3:T(8,128)S(1)} %bitcast.37), kind=kOutput, calls=%fused_computation | convolution fusion | flops 169869312 | bytes 8651904 | tf_op jit(solution)/shard_map/dot_general | solution.py:104
  81.4 6.3 %collective-permute-start.2 = (bf16[8,6,32,128]{3,0,2,1:T(8,128)(2,1)S(1)}, bf16[8,6,32,128]{3,0,2,1:T(8,128)(2,1)S(1)}, u32[]{:S(2)}, u32[]{:S(2)}) collective-permute-start(bf16[8,6,32,128]{3,0,2,1:T(8,128)(2,1)S(1)} %slice.432), channel_id=1, source_target_pairs={{0,8},{8,16},{16,24},{24,32},{32,40},{40,48},{48,56},{56,64},{64,7... | collective-permute-start | bytes 1179656 | tf_op jit(solution)/shard_map/ppermute | solution.py:50
  87.7 1.5 fusion.59
  89.1 16.4 %collective-permute-done.2 = bf16[8,6,32,128]{3,0,2,1:T(8,128)(2,1)S(1)} collective-permute-done((bf16[8,6,32,128]{3,0,2,1:T(8,128)(2,1)S(1)}, bf16[8,6,32,128]{3,0,2,1:T(8,128)(2,1)S(1)}, u32[]{:S(2)}, u32[]{:S(2)}) %collective-permute-start.2) | collective-permute-done | bytes 393248 | tf_op jit(solution)/shard_map/ppermute | solution.py:50
  106.3 11.9 %fusion.8 = bf16[8,6,32,128]{3,0,2,1:T(8,128)(2,1)S(1)} fusion(f32[8,12,32,128]{3,0,2,1:T(8,128)S(1)} %fusion, f32[8,12,32,128]{3,0,2,1:T(8,128)S(1)} %get-tuple-element.60, f32[8,12,32,128]{3,0,2,1:T(8,128)S(1)} %constant_dynamic-update-slice_fusion, f32[8,6,31,128]{3,0,2,1:T(8,128)} %get-tuple-element.57, f32[8,6,1,128]{3,0,2,1:T(8,128)S(1)} %get-tuple-element.59, ...), kind=kLoop, calls=%fused_computation.13 | loop fusion | flops 18087936 | bytes 31555584 | tf_op jit(solution)/shard_map/convert_element_type | solution.py:116
  118.3 2.4 stack.2
  120.7 16.5 %all-to-all-start = ((bf16[8,8,6,32,128]{4,3,2,1,0:T(8,128)(2,1)}), bf16[8,8,6,32,128]{4,3,2,1,0:T(8,128)(2,1)}, u32[]{:S(2)}, u32[]{:S(2)}) async-start(bf16[8,8,6,32,128]{4,3,2,1,0:T(8,128)(2,1)} %stack.2), calls=%async_computation | async-start | bytes 6291456 | tf_op jit(solution)/shard_map/all_to_all | solution.py:26
  139.2 66.2 %all-to-all-done = bf16[8,8,6,32,128]{4,3,2,1,0:T(8,128)(2,1)} async-done(((bf16[8,8,6,32,128]{4,3,2,1,0:T(8,128)(2,1)}), bf16[8,8,6,32,128]{4,3,2,1,0:T(8,128)(2,1)}, u32[]{:S(2)}, u32[]{:S(2)}) %all-to-all-start) | async-done | bytes 3145760 | tf_op jit(solution)/shard_map/all_to_all | solution.py:26
  205.3 4.7 %reshape_reshape.3 = bf16[64,24576]{1,0:T(8,128)(2,1)} reshape(bf16[8,8,6,32,128]{4,3,2,1,0:T(8,128)(2,1)} %all-to-all-done) | data formatting | bytes 6291456 | tf_op jit(solution)/shard_map/reshape;reshape | solution.py:122
  210.1 3.0 convolution_multiply_fusion
  213.1 220.5 %all-reduce = f32[64,16]{1,0:T(8,128)S(1)} all-reduce(f32[64,16]{1,0:T(8,128)S(1)} %convolution_multiply_fusion), channel_id=2, replica_groups=mesh['space'=32,'band'=8] {'space'}, use_global_device_ids=true, to_apply=%region_0.1.clone | all-reduce | flops 1024 | bytes 8192
  (69 shorter events, 26.9 us)
Async XLA Ops:
  0.6 35.8 %copy-start = (bf16[4,9,6,32,128]{4,3,2,1,0:T(8,128)(2,1)S(1)}, bf16[4,9,6,32,128]{4,3,2,1,0:T(8,128)(2,1)}, u32[]{:S(2)}) copy-start(bf16[4,9,6,32,128]{4,3,2,1,0:T(8,128)(2,1)} %param.9) | copy-start | bytes 5308420
  2.4 59.7 %collective-permute-start.1 = (f32[8,6,32,128]{3,0,2,1:T(8,128)S(1)}, f32[8,6,32,128]{3,0,2,1:T(8,128)S(1)}, u32[]{:S(2)}, u32[]{:S(2)}) collective-permute-start(f32[8,6,32,128]{3,0,2,1:T(8,128)S(1)} %copy.131), channel_id=1, source_target_pairs={{0,8},{8,16},{16,24},{24,32},{32,40},{40,48},{48,56},{56,64},{64,7... | collective-permute-start | bytes 2359304 | tf_op jit(solution)/shard_map/ppermute | solution.py:39
  8.7 57.0 %collective-permute-start = (f32[8,6,32,128]{3,0,2,1:T(8,128)S(1)}, f32[8,6,32,128]{3,0,2,1:T(8,128)}, u32[]{:S(2)}, u32[]{:S(2)}) collective-permute-start(f32[8,6,32,128]{3,0,2,1:T(8,128)S(1)} %copy.131), channel_id=1, source_target_pairs={{8,0},{16,8},{24,16},{32,24},{40,32},{48,40},{56,48},{64,56},{72,6... | collective-permute-start | bytes 2359304 | tf_op jit(solution)/shard_map/ppermute | solution.py:42
  34.8 1.5 copy-start.12
  51.9 1.5 copy-start.11
  58.2 8.7 %slice-start = ((s8[7864320]{0:T(1024)(128)(4,1)}), s8[4194304]{0:T(1024)(128)(4,1)S(1)}, s32[]{:S(2)}) async-start(s8[7864320]{0:T(1024)(128)(4,1)} %bitcast.35), calls=%async_computation.1 | async-start | bytes 8388608
  58.3 8.7 %slice-start.1 = ((s8[7864320]{0:T(1024)(128)(4,1)}), s8[3670016]{0:T(1024)(128)(4,1)S(1)}, s32[]{:S(2)}) async-start(s8[7864320]{0:T(1024)(128)(4,1)} %bitcast.35), calls=%async_computation.2 | async-start | bytes 7340032
  59.0 3.1 copy-start.2
  81.3 25.0 %copy-start.7 = (f32[8,6,32,126]{3,0,2,1:T(8,128)S(1)}, f32[8,6,32,126]{3,0,2,1:T(8,128)}, u32[]{:S(2)}) copy-start(f32[8,6,32,126]{3,0,2,1:T(8,128)} %get-tuple-element.28) | copy-start | bytes 2322436
  81.3 25.0 %copy-start.3 = (f32[8,6,32,127]{3,0,2,1:T(8,128)S(1)}, f32[8,6,32,127]{3,0,2,1:T(8,128)}, u32[]{:S(2)}) copy-start(f32[8,6,32,127]{3,0,2,1:T(8,128)} %get-tuple-element.32) | copy-start | bytes 2340868
  81.3 25.0 %copy-start.4 = (f32[8,6,32,127]{3,0,2,1:T(8,128)S(1)}, f32[8,6,32,127]{3,0,2,1:T(8,128)}, u32[]{:S(2)}) copy-start(f32[8,6,32,127]{3,0,2,1:T(8,128)} %get-tuple-element.33) | copy-start | bytes 2340868
  81.3 25.0 %copy-start.5 = (f32[8,6,32,1]{3,0,2,1:T(8,128)S(1)}, f32[8,6,32,1]{3,0,2,1:T(8,128)}, u32[]{:S(2)}) copy-start(f32[8,6,32,1]{3,0,2,1:T(8,128)} %get-tuple-element.34) | copy-start | bytes 18436
  81.4 25.0 %copy-start.6 = (f32[8,6,32,1]{3,0,2,1:T(8,128)S(1)}, f32[8,6,32,1]{3,0,2,1:T(8,128)}, u32[]{:S(2)}) copy-start(f32[8,6,32,1]{3,0,2,1:T(8,128)} %get-tuple-element.35) | copy-start | bytes 18436
  81.4 25.0 %copy-start.9 = (f32[8,6,6,128]{3,0,2,1:T(8,128)S(1)}, f32[8,6,6,128]{3,0,2,1:T(8,128)}, u32[]{:S(2)}) copy-start(f32[8,6,6,128]{3,0,2,1:T(8,128)} %get-tuple-element.39) | copy-start | bytes 442372
  81.4 24.2 %collective-permute-start.2 = (bf16[8,6,32,128]{3,0,2,1:T(8,128)(2,1)S(1)}, bf16[8,6,32,128]{3,0,2,1:T(8,128)(2,1)S(1)}, u32[]{:S(2)}, u32[]{:S(2)}) collective-permute-start(bf16[8,6,32,128]{3,0,2,1:T(8,128)(2,1)S(1)} %slice.432), channel_id=1, source_target_pairs={{0,8},{8,16},{16,24},{24,32},{32,40},{40,48},{48,56},{56,64},{64,7... | collective-permute-start | bytes 1179656 | tf_op jit(solution)/shard_map/ppermute | solution.py:50
  105.6 0.7 copy-start.10
  118.3 2.5 copy-start.8
  120.7 84.6 %all-to-all-start = ((bf16[8,8,6,32,128]{4,3,2,1,0:T(8,128)(2,1)}), bf16[8,8,6,32,128]{4,3,2,1,0:T(8,128)(2,1)}, u32[]{:S(2)}, u32[]{:S(2)}) async-start(bf16[8,8,6,32,128]{4,3,2,1,0:T(8,128)(2,1)} %stack.2), calls=%async_computation | async-start | bytes 6291456 | tf_op jit(solution)/shard_map/all_to_all | solution.py:26
  137.3 0.7 copy-start.13
  210.1 224.2 %copy-start.1 = (bf16[4,9,6,32,128]{4,3,2,1,0:T(8,128)(2,1)S(1)}, bf16[4,9,6,32,128]{4,3,2,1,0:T(8,128)(2,1)}, u32[]{:S(2)}) copy-start(bf16[4,9,6,32,128]{4,3,2,1,0:T(8,128)(2,1)} %param.9) | copy-start | bytes 5308420
